TPU v7x, 32 devices: a whole 2x2x4 slice. The times are simulated.
32 devices in a mesh: groups: 2 (over y), seq: 4 (over z), tensor: 4 (over x, core).
Axes of the slice: x: 2, y: 2, z: 4, core: 2. Of those that a mesh axis runs over, the one named last changes fastest.
Arguments:
- activations: bfloat16 [2048, 4096], P(('groups', 'seq')), parts along dimension 0, may hold values from -6 to 6
- token_adapter_index: int32 [2048], P(('groups', 'seq')), parts along dimension 0, may hold values from 0 to 15
- gate_scanned_weight: bfloat16 [4096, 2, 8192], P('seq', None, 'tensor'), may hold values from -0.09375 to 0.09375
- state_vector_weight: bfloat16 [4096, 2, 1024], P('seq'), may hold values from -0.09375 to 0.09375
- time_step_weight: bfloat16 [4096, 128], P('seq', 'tensor'), may hold values from -0.09375 to 0.09375
- adapter_down_maps: bfloat16 [4096, 256], P('seq'), may hold values from -0.09375 to 0.09375
- adapter_up_maps: bfloat16 [256, 2, 8192], P(None, None, 'tensor'), may hold values from -1.5 to 1.5
- scanned_channel_taps: float32 [4, 8192], P(None, 'tensor'), may hold values from -3 to 3
- state_vector_taps: float32 [4, 2, 1024], replicated, may hold values from -3 to 3
- earlier_scanned_channels: bfloat16 [6, 8192], P('groups', 'tensor'), parts along dimension 0, may hold values from -6 to 6
- earlier_state_vectors: bfloat16 [6, 2, 1024], P('groups'), parts along dimension 0, may hold values from -6 to 6
- head_step_bias: float32 [128], P('tensor'), may hold values from -4 to -1
- adapter_step_shift: float32 [16, 128], P(None, 'tensor'), may hold values from -3 to 3
- head_decay_rate: float32 [128], P('tensor'), may hold values from 0.0001953125 to 0.3
- starting_head_state: float32 [256, 64, 128], P(('groups', 'tensor')), parts along dimension 0, may hold values from -6 to 6
- gated_norm_gain: float32 [8192], P('tensor'), may hold values from 0.1 to 1.9
- output_projection_weight: bfloat16 [8192, 4096], P('tensor', 'seq'), may hold values from -0.0625 to 0.0625
Outputs:
- mixed: bfloat16 [2048, 4096], P(('groups', 'tensor'), 'seq'), parts along dimension 0
- checkpoints: float32 [8, 128, 64, 128], P(('groups', 'seq'), 'tensor'), parts along dimension 0
There are 2 independent parts, one for each index of `groups`. A program takes and returns all parts, laid end to end along the dimension named above; an argument that names none is the same for every part. Nothing has to cross between parts.
All inputs are finite; a program needn't handle non-finite values.
Results may differ from a plain program's by a relative error of at most 0.02.
Values may be sent and summed in bfloat16 or wider, within the bound.
No kernel may reach another device: no remote copies, remote signals or barrier semaphores. Data moves between devices by JAX's collectives and lax.ppermute only.
A program may use at most 192 MiB of HBM per device.

v0:
```python
import jax
import jax.numpy as jnp
from jax import lax
from jax.sharding import PartitionSpec as P

HEADS = 128
HEAD_DIM = 64
STATE = 128
HEAD_SETS = 8
ADAPTER_COUNT = 16
ADAPTER_RANK = 16
CONV = 4
BLOCK = 128


def passed_along(array, axis, by):
    peers = lax.axis_size(axis)
    pairs = [(i, i + by) for i in range(peers) if 0 <= i + by < peers]
    return lax.ppermute(array, axis, pairs)


def entering_2(array, axis, join, neutral):
    place = lax.axis_index(axis)
    gathered = jax.tree.map(
        lambda a, kind: lax.all_gather(a.astype(kind), axis),
        array,
        jax.tree.map(lambda a: jnp.bfloat16 if a.dtype == jnp.float32 else a.dtype, array),
    )
    state = jax.tree.map(lambda a, e: jnp.zeros_like(a) + jnp.asarray(e, a.dtype), array, neutral)

    def one(lap, state):
        return join(
            state,
            jax.tree.map(
                lambda a, own: lax.dynamic_index_in_dim(a, lap, 0, False).astype(own.dtype),
                gathered,
                array,
            ),
        )

    return lax.fori_loop(0, place, one, state)


def settle(value):
    return lax.optimization_barrier(value.astype(jnp.bfloat16))


def causal_conv(series, prior, kernel):
    count = series.shape[0]
    padded = jnp.concatenate([prior, series], axis=0).astype(jnp.float32)
    total = jnp.zeros(series.shape, jnp.float32)
    for offset in range(CONV):
        total = total + kernel[offset] * padded[offset : offset + count]
    return settle(jax.nn.silu(total))


def join_states(earlier, later):
    return (earlier[0] + later[0], jnp.exp(later[0])[:, None, None] * earlier[1] + later[1])


def per_device(
    activations,
    token_adapter_index,
    gate_scanned_weight,
    state_vector_weight,
    time_step_weight,
    adapter_down_maps,
    adapter_up_maps,
    scanned_channel_taps,
    state_vector_taps,
    earlier_scanned_channels,
    earlier_state_vectors,
    head_step_bias,
    adapter_step_shift,
    head_decay_rate,
    starting_head_state,
    gated_norm_gain,
    output_projection_weight,
):
    tokens_here = activations.shape[0]
    heads_here = time_step_weight.shape[1]
    local_inner_channels = gate_scanned_weight.shape[2]
    per_set = HEADS // HEAD_SETS
    sets_here = max(1, heads_here // per_set)
    heads_per = heads_here // sets_here
    first_set = lax.axis_index("tensor") * heads_here // per_set
    io_start = first_set * STATE
    io_width = sets_here * STATE
    mine_io = lax.dynamic_slice_in_dim(state_vector_weight, io_start, io_width, 2)
    kernel_io = lax.dynamic_slice_in_dim(state_vector_taps, io_start, io_width, 2).reshape(
        CONV, 2 * io_width
    )
    prior_io = lax.dynamic_slice_in_dim(earlier_state_vectors, io_start, io_width, 2).reshape(
        CONV - 1, 2 * io_width
    )
    owner_adapter = jnp.arange(ADAPTER_COUNT * ADAPTER_RANK, dtype=jnp.int32) // ADAPTER_RANK
    chosen = token_adapter_index[:, None] == owner_adapter[None, :]
    chosen_up_weight = adapter_up_maps.reshape(
        ADAPTER_COUNT * ADAPTER_RANK, 2 * local_inner_channels
    )

    def add_product(piece):
        return jnp.dot(
            activations, piece.reshape(piece.shape[0], -1), preferred_element_type=jnp.float32
        )

    pieces = (
        lax.all_gather(gate_scanned_weight, "seq", axis=0, tiled=True),
        lax.all_gather(mine_io, "seq", axis=0, tiled=True),
        lax.all_gather(time_step_weight, "seq", axis=0, tiled=True),
        lax.all_gather(adapter_down_maps, "seq", axis=0, tiled=True),
    )
    pair_raw, io_raw, step_raw, adapter_hidden = tuple(
        (add_product(pieces[index]) for index in range(len(pieces)))
    )
    adapter_hidden = settle(jnp.where(chosen, adapter_hidden, 0.0))
    pair_raw = pair_raw + jnp.dot(
        adapter_hidden, chosen_up_weight, preferred_element_type=jnp.float32
    )
    gate_and_scanned = settle(pair_raw).reshape(tokens_here, 2, local_inner_channels)
    gate_values = gate_and_scanned[:, 0]
    mix_values = gate_and_scanned[:, 1]
    state_io = settle(io_raw)
    rim_rows = passed_along(
        (mix_values[tokens_here - (CONV - 1) :], state_io[tokens_here - (CONV - 1) :]), "seq", 1
    )
    at_start = lax.axis_index("seq") == 0
    rim_mix = jnp.where(at_start, earlier_scanned_channels, rim_rows[0])
    rim_io = jnp.where(at_start, prior_io, rim_rows[1])
    mix_conv = causal_conv(mix_values, rim_mix, scanned_channel_taps)
    state_conv = causal_conv(state_io, rim_io, kernel_io).reshape(tokens_here, 2, sets_here, STATE)
    onehot = (
        token_adapter_index[:, None] == jnp.arange(ADAPTER_COUNT, dtype=jnp.int32)[None, :]
    ).astype(jnp.float32)
    shift_here = jnp.dot(
        onehot,
        adapter_step_shift,
        precision=lax.Precision.HIGHEST,
        preferred_element_type=jnp.float32,
    )
    timestep = jax.nn.softplus(step_raw + head_step_bias + shift_here)
    blocks = tokens_here // BLOCK
    mix_blocks = mix_conv.reshape(blocks, BLOCK, heads_here, HEAD_DIM)
    input_blocks = state_conv[:, 0].reshape(blocks, BLOCK, sets_here, STATE)
    output_blocks = state_conv[:, 1].reshape(blocks, BLOCK, sets_here, STATE)
    step_blocks = timestep.reshape(blocks, BLOCK, heads_here)
    cumulative = jnp.cumsum(-head_decay_rate * step_blocks, axis=1)
    scores = jnp.einsum(
        "bign,bjgn->bgij", output_blocks, input_blocks, preferred_element_type=jnp.float32
    )
    scores = jnp.repeat(scores, heads_per, axis=1)
    cum_heads = jnp.swapaxes(cumulative, 1, 2)
    gaps = cum_heads[:, :, :, None] - cum_heads[:, :, None, :]
    row_index = lax.broadcasted_iota(jnp.int32, (BLOCK, BLOCK), 0)
    col_index = lax.broadcasted_iota(jnp.int32, (BLOCK, BLOCK), 1)
    causal = row_index >= col_index
    weight = jnp.where(causal, jnp.exp(jnp.minimum(gaps, 0.0)), 0.0)
    mixing = settle(scores * weight * jnp.swapaxes(step_blocks, 1, 2)[:, :, None, :])
    intra_out = jnp.einsum(
        "bhij,bjhp->bihp", mixing, mix_blocks, preferred_element_type=jnp.float32
    )
    input_heads = jnp.repeat(input_blocks, heads_per, axis=2)
    output_heads = jnp.repeat(output_blocks, heads_per, axis=2)
    block_total = cumulative[:, -1]
    scaled = settle(
        mix_blocks.astype(jnp.float32)
        * (step_blocks * jnp.exp(block_total[:, None, :] - cumulative))[..., None]
    )
    update = jnp.einsum("bjhp,bjhn->bhpn", scaled, input_heads, preferred_element_type=jnp.float32)
    empty_decay = jnp.zeros((heads_here,), jnp.float32)
    empty_state = jnp.zeros((heads_here, HEAD_DIM, STATE), jnp.float32)
    carried = (empty_decay, empty_state)
    prefix_decay = []
    prefix_state = []
    for block in range(blocks):
        prefix_decay.append(carried[0])
        prefix_state.append(carried[1])
        carried = join_states(carried, (block_total[block], update[block]))
    before = entering_2(carried, "seq", join_states, (empty_decay, empty_state))
    entering = jnp.exp(before[0])[:, None, None] * starting_head_state + before[1]
    block_states = jnp.exp(jnp.stack(prefix_decay))[:, :, None, None] * entering[None] + jnp.stack(
        prefix_state
    )
    inter_out = jnp.exp(cumulative)[..., None] * jnp.einsum(
        "bihn,bhpn->bihp",
        output_heads.astype(jnp.float32),
        block_states,
        precision=lax.Precision.HIGHEST,
    )
    finish = jnp.exp(carried[0])[:, None, None] * entering + carried[1]
    scan_out = (intra_out + inter_out).reshape(tokens_here, local_inner_channels)
    gated = settle(scan_out * jax.nn.silu(gate_values.astype(jnp.float32)))
    gathered = lax.all_gather(gated, "seq", axis=0, tiled=True)
    squares = jnp.sum(jnp.square(gathered.astype(jnp.float32)), axis=1)
    hidden = settle(gathered.astype(jnp.float32) * gated_norm_gain)
    partial_sum = jnp.dot(hidden, output_projection_weight, preferred_element_type=jnp.float32)
    summed, total_squares = (
        lax.psum_scatter(
            partial_sum.astype(jnp.bfloat16), "tensor", scatter_dimension=0, tiled=True
        ).astype(jnp.float32),
        lax.psum_scatter(
            squares.astype(jnp.bfloat16), "tensor", scatter_dimension=0, tiled=True
        ).astype(jnp.float32),
    )
    mixed = (summed * lax.rsqrt(total_squares / (HEADS * HEAD_DIM) + 1e-05)[:, None]).astype(
        jnp.bfloat16
    )
    return (mixed, finish[None])


def solution(mesh):
    return jax.shard_map(
        per_device,
        mesh=mesh,
        in_specs=(
            P(("groups", "seq"), None),
            P(("groups", "seq")),
            P("seq", None, "tensor"),
            P("seq", None, None),
            P("seq", "tensor"),
            P("seq", None),
            P(None, None, "tensor"),
            P(None, "tensor"),
            P(),
            P("groups", "tensor"),
            P("groups", None, None),
            P("tensor"),
            P(None, "tensor"),
            P("tensor"),
            P(("groups", "tensor"), None, None),
            P("tensor"),
            P("tensor", "seq"),
        ),
        out_specs=(P(("groups", "tensor"), "seq"), P(("groups", "seq"), "tensor", None, None)),
        check_vma=False,
    )
```

profile of v0, /device:TPU:0, one launch (start us, length us, event | category | flops | bytes accessed | tf_op | source)
XLA Modules:
  0.0 960.9 jit_solution(7413483118449499834)
XLA Ops:
  7.2 3.1 constant_dynamic-slice_fusion.1
  10.4 0.7 all-gather.9.cloned.1.call-update
  11.2 0.7 all-gather.7.cloned.1.call-update
  11.9 0.7 dynamic-slice_bitcast_fusion.3
  12.7 0.7 constant_dynamic-slice_fusion.2
  13.6 17.2 %all_gather.26 = bf16[4096,32]{0,1:T(8,128)(2,1)S(1)} all-gather(bf16[1024,32]{0,1:T(8,128)(2,1)S(1)} %copy-done.14), channel_id=1, replica_groups=mesh['groups'=2,'seq'=4,'tensor'=4] {'seq'}, dimensions={0}, use_global_device_ids=true | all-gather | bytes 327680 | tf_op jit(solution)/shard_map/all_gather | solution.py:110
  30.8 0.7 convolution_add_fusion.2
  31.6 0.3 compare_select_fusion
  31.9 0.6 copy-done.10
  32.8 0.7 fusion.37
  33.5 0.7 copy.65
  34.2 0.3 copy.51
  34.5 3.9 copy.76
  38.4 0.6 slice_bitcast_fusion.3
  39.0 0.6 fusion.38
  39.6 56.1 %all-gather.11.cloned.1.call-done = bf16[4096,2,256]{2,1,0:T(2,128)(2,1)} async-done(((bf16[1024,2,256]{2,1,0:T(2,128)(2,1)}), bf16[4096,2,256]{2,1,0:T(2,128)(2,1)}) %all-gather.11.cloned.1.call-update) | async-done | bytes 4194320 | tf_op jit(solution)/shard_map/all_gather | solution.py:109
  95.7 2.9 copy.78
  98.6 1.3 fusion.16
  100.0 1.5 collective-permute-start.1
  101.5 40.3 %all-gather.9.cloned.1.call-done = bf16[4096,256]{1,0:T(8,128)(2,1)} async-done(((bf16[1024,256]{1,0:T(8,128)(2,1)}), bf16[4096,256]{1,0:T(8,128)(2,1)}) %all-gather.9.cloned.1.call-update) | async-done | bytes 2097168 | tf_op jit(solution)/shard_map/all_gather | solution.py:111
  141.8 3.0 fusion.17
  144.9 0.8 multiply_convert_fusion.4
  145.7 0.7 fusion.36
  146.5 557.4 %all-gather.7.cloned.1.call-done = bf16[4096,2,2048]{2,1,0:T(2,128)(2,1)} async-done(((bf16[1024,2,2048]{2,1,0:T(2,128)(2,1)}), bf16[4096,2,2048]{2,1,0:T(2,128)(2,1)}) %all-gather.7.cloned.1.call-update) | async-done | bytes 33554448 | tf_op jit(solution)/shard_map/all_gather | solution.py:108
  703.9 23.2 %copy.75 = bf16[512,8,2,2048]{3,1,2,0:T(8,128)(2,1)} copy(bf16[512,8,2,2048]{3,2,1,0:T(2,128)(2,1)} %bitcast.126) | data formatting | bytes 67108864
  727.1 15.2 %fusion.39 = f32[256,4096]{1,0:T(8,128)S(1)} fusion(bf16[256,4096]{1,0:T(8,128)(2,1)S(1)} %copy-done, bf16[4096,4096]{1,0:T(8,128)(2,1)} %bitcast.127), kind=kOutput, calls=%fused_computation.102 | convolution fusion | flops 8589934592 | bytes 39845888 | tf_op jit(solution)/shard_map/dot_general | solution.py:103
  742.3 2.1 fusion.2
  744.4 3.3 copy.71
  747.7 0.2 slice_bitcast_fusion.2
  747.9 1.3 collective-permute-start
  749.3 11.5 %collective-permute-done = bf16[3,2048]{0,1:T(8,128)(2,1)S(1)} collective-permute-done((bf16[3,2048]{0,1:T(8,128)(2,1)S(1)}, bf16[3,2048]{0,1:T(8,128)(2,1)S(1)}, u32[]{:S(2)}, u32[]{:S(2)}) %collective-permute-start) | collective-permute-done | bytes 12320 | tf_op jit(solution)/shard_map/ppermute | solution.py:19
  760.9 0.7 maximum_convert_fusion
  761.6 3.2 multiply_convert_fusion.2
  764.8 0.3 reshape.151
  765.1 0.5 copy-done.13
  765.6 1.1 multiply_convert_fusion.1
  766.6 0.5 broadcast_in_dim.31
  767.2 0.7 fusion.21
  767.9 1.6 add_convert_fusion
  769.7 0.8 copy.61
  770.5 10.9 %all-gather = bf16[4,1,32]{2,1,0:T(2,128)(2,1)S(1)} all-gather(bf16[1,1,32]{2,1,0:T(2,128)(2,1)S(1)} %fusion.31), channel_id=1, replica_groups=mesh['groups'=2,'seq'=4,'tensor'=4] {'seq'}, dimensions={0}, use_global_device_ids=true | all-gather | bytes 320 | tf_op jit(solution)/shard_map/all_gather | solution.py:25
  781.4 0.7 copy.63
  782.1 0.6 pad_exponential_fusion
  782.8 1.0 copy.73
  784.1 0.5 broadcast_in_dim.26
  784.6 2.8 multiply_convert_fusion
  787.4 28.9 %all-gather.13.cloned.1.call-done = bf16[4,32,64,128]{3,2,1,0:T(8,128)(2,1)} async-done(((bf16[1,32,64,128]{3,2,1,0:T(8,128)(2,1)}), bf16[4,32,64,128]{3,2,1,0:T(8,128)(2,1)}) %all-gather.13.cloned.1.call-update) | async-done | bytes 2097168 | tf_op jit(solution)/shard_map/all_gather | solution.py:25
  816.4 1.2 copy-done.8
  817.6 2.9 fusion.19
  820.5 0.5 broadcast_in_dim.32
  821.0 0.7 copy-done.7
  821.7 4.2 fusion.11
  825.9 1.5 fusion.10
  827.5 1.7 copy.69
  829.2 1.7 fusion.15
  830.9 82.3 %all-gather.15.cloned.1.call-done = bf16[1024,2048]{0,1:T(8,128)(2,1)} async-done(((bf16[256,2048]{0,1:T(8,128)(2,1)}), bf16[1024,2048]{0,1:T(8,128)(2,1)}) %all-gather.15.cloned.1.call-update) | async-done | bytes 4194320 | tf_op jit(solution)/shard_map/all_gather | solution.py:193
  913.3 3.0 fusion.1
  916.3 0.4 copy-done.24
  916.7 5.8 convolution_convert_fusion
  922.6 0.6 copy-done.28
  923.2 0.6 dynamic-slice
  924.4 6.8 all-reduce.2
  931.4 20.7 %reduce-scatter.2.cloned.1.call-done = bf16[256,1024]{1,0:T(8,128)(2,1)} async-done(((bf16[1024,1024]{1,0:T(8,128)(2,1)}), bf16[256,1024]{1,0:T(8,128)(2,1)}) %reduce-scatter.2.cloned.1.call-update) | async-done | bytes 524304 | tf_op jit(solution)/shard_map/reduce_scatter | solution.py:198
  952.1 2.0 multiply_convert_fusion.3
  (93 shorter events, 2.2 us)
Async XLA Ops:
  7.2 23.7 %copy-start = (bf16[256,4096]{1,0:T(8,128)(2,1)S(1)}, bf16[256,4096]{1,0:T(8,128)(2,1)}, u32[]{:S(2)}) copy-start(bf16[256,4096]{1,0:T(8,128)(2,1)} %param.19) | copy-start | bytes 6291460
  7.2 88.5 %all-gather.11.cloned.1.call-start = ((), (), s32[]{:S(2)}) async-start(), calls=%async_computation.3 | async-start | bytes 5242880 | tf_op jit(solution)/shard_map/all_gather | solution.py:109
  10.3 131.4 %all-gather.9.cloned.1.call-start = ((), (), s32[]{:S(2)}) async-start(), calls=%async_computation.2 | async-start | bytes 2621440 | tf_op jit(solution)/shard_map/all_gather | solution.py:111
  11.1 0.9 copy-start.27
  11.1 2.5 copy-start.14
  11.1 19.7 %copy-start.23 = (f32[32]{0:T(128)S(1)}, f32[32]{0:T(128)}, u32[]{:S(2)}) copy-start(f32[32]{0:T(128)} %param.30) | copy-start | bytes 388
  11.1 692.8 %all-gather.7.cloned.1.call-start = ((), (), s32[]{:S(2)}) async-start(), calls=%async_computation.1 | async-start | bytes 41943040 | tf_op jit(solution)/shard_map/all_gather | solution.py:108
  11.8 19.7 %copy-start.25 = (f32[16,32]{1,0:T(8,128)S(1)}, f32[16,32]{1,0:T(8,128)}, u32[]{:S(2)}) copy-start(f32[16,32]{1,0:T(8,128)} %param.31) | copy-start | bytes 6148
  11.9 19.7 %copy-start.26 = (s32[256]{0:T(256)S(1)}, s32[256]{0:T(256)}, u32[]{:S(2)}) copy-start(s32[256]{0:T(256)} %param.20) | copy-start | bytes 3076
  11.9 804.4 %all-gather.13.cloned.1.call-start = ((), (), s32[]{:S(2)}) async-start(), calls=%async_computation.4 | async-start | bytes 2621440 | tf_op jit(solution)/shard_map/all_gather | solution.py:25
  13.6 20.6 %copy-start.18 = (bf16[3,2048]{1,0:T(4,128)(2,1)S(1)}, bf16[3,2048]{1,0:T(4,128)(2,1)}, u32[]{:S(2)}) copy-start(bf16[3,2048]{1,0:T(4,128)(2,1)} %param.28) | copy-start | bytes 36868
  31.9 0.6 copy-start.10
  34.5 4.4 copy-start.17
  100.0 44.7 %collective-permute-start.1 = (bf16[3,512]{0,1:T(8,128)(2,1)S(1)}, bf16[3,512]{0,1:T(8,128)(2,1)S(1)}, u32[]{:S(2)}, u32[]{:S(2)}) collective-permute-start(bf16[3,512]{0,1:T(8,128)(2,1)S(1)} %slice.130), channel_id=1, source_target_pairs={{0,4},{4,8},{8,12},{1,5},{5,9},{9,13},{2,6},{6,10},{10,14},{3,7},{... | collective-permute-start | bytes 9224 | tf_op jit(solution)/shard_map/ppermute | solution.py:19
  727.1 15.2 %copy-start.6 = (bf16[32,8,2,2048]{3,1,2,0:T(8,128)(2,1)S(1)}, bf16[32,8,2,2048]{3,1,2,0:T(8,128)(2,1)}, u32[]{:S(2)}) copy-start(bf16[32,8,2,2048]{3,1,2,0:T(8,128)(2,1)} %copy.76) | copy-start | bytes 6291460
  727.1 15.2 %copy-start.11 = (bf16[256,256]{1,0:T(8,128)(2,1)S(1)}, bf16[256,256]{1,0:T(8,128)(2,1)}, u32[]{:S(2)}) copy-start(bf16[256,256]{1,0:T(8,128)(2,1)} %fusion.17) | copy-start | bytes 393220
  747.7 13.2 %copy-start.3 = (bf16[256,4096]{0,1:T(8,128)(2,1)}, bf16[256,4096]{0,1:T(8,128)(2,1)S(1)}, u32[]{:S(2)}) copy-start(bf16[256,4096]{0,1:T(8,128)(2,1)S(1)} %copy.71) | copy-start | bytes 6291460
  747.9 12.9 %collective-permute-start = (bf16[3,2048]{0,1:T(8,128)(2,1)S(1)}, bf16[3,2048]{0,1:T(8,128)(2,1)S(1)}, u32[]{:S(2)}, u32[]{:S(2)}) collective-permute-start(bf16[3,2048]{0,1:T(8,128)(2,1)S(1)} %slice_bitcast_fusion.2), channel_id=1, source_target_pairs={{0,4},{4,8},{8,12},{1,5},{5,9},{9,13},{2,6},{6,10},{10,14},{3,7},{... | collective-permute-start | bytes 36872 | tf_op jit(solution)/shard_map/ppermute | solution.py:19
  760.9 0.7 copy-start.15
  760.9 0.7 copy-start.16
  764.8 0.8 copy-start.13
  767.1 0.7 copy-start.20
  767.2 0.7 copy-start.21
  767.9 1.9 copy-start.2
  767.9 13.5 %copy-start.9 = (f32[2,128,32]{2,1,0:T(8,128)S(1)}, f32[2,128,32]{2,1,0:T(8,128)}, u32[]{:S(2)}) copy-start(f32[2,128,32]{2,1,0:T(8,128)} %get-tuple-element.60) | copy-start | bytes 98308
  769.7 143.5 %all-gather.15.cloned.1.call-start = ((), (), s32[]{:S(2)}) async-start(), calls=%async_computation.5 | async-start | bytes 5242880 | tf_op jit(solution)/shard_map/all_gather | solution.py:193
  816.4 1.2 copy-start.8
  816.4 1.2 copy-start.22
  820.5 1.2 copy-start.7
  821.7 4.2 copy-start.5
  821.7 4.2 copy-start.12
  827.5 1.7 copy-start.4
  829.2 84.1 %copy-start.19 = (f32[2048]{0:T(1024)S(1)}, f32[2048]{0:T(1024)}, u32[]{:S(2)}) copy-start(f32[2048]{0:T(1024)} %param.34) | copy-start | bytes 24580
  830.9 121.2 %reduce-scatter.2.cloned.1.call-start = ((), (), s32[]{:S(2)}) async-start(), calls=%async_computation.6 | async-start | bytes 2621440 | tf_op jit(solution)/shard_map/reduce_scatter | solution.py:198
  913.3 3.4 copy-start.24
  916.7 37.3 %copy-start.1 = (bf16[256,4096]{1,0:T(8,128)(2,1)S(1)}, bf16[256,4096]{1,0:T(8,128)(2,1)}, u32[]{:S(2)}) copy-start(bf16[256,4096]{1,0:T(8,128)(2,1)} %param.19) | copy-start | bytes 6291460
  922.5 0.7 copy-start.28
Sparse Core Ops, SparseCore 0:
  10.4 85.1 all-gather.10
  97.2 44.4 all-gather.8
  143.3 560.5 all-gather.6
  769.7 46.5 all-gather.12
  831.0 82.2 all-gather.14
  922.7 29.3 reduce-scatter.1
where the time goes:
time: 962 us; the launch traced here: 961 us
  waiting for transfers between devices  799 us (83%)
  local copies, waits for them, and re-layouts  52.5 us (5%)
  matrix products  35 us (4%)
  blocking collectives  34.9 us (4%)
  other arithmetic  21.6 us (2%)
  between operations  15.3 us (2%)
    all_gather x1, waiting for transfers between devices, per_device(): lax.all_gather(gate_scanned_weight, 'seq', axis=0, tiled=True)  557 us
    all_gather x1, waiting for transfers between devices, per_device(): gathered = lax.all_gather(gated, 'seq', axis=0, tiled=True)  82.3 us
    all_gather x1, waiting for transfers between devices, per_device(): lax.all_gather(mine_io, 'seq', axis=0, tiled=True)  56.1 us
    all_gather x1, waiting for transfers between devices, per_device(): lax.all_gather(adapter_down_maps, 'seq', axis=0, tiled=True)  40.3 us
    unnamed x71, local copies, waits for them, and re-layouts  37 us
    all_gather x1, waiting for transfers between devices, entering_2(): lax.all_gather(a.astype(kind), axis)  28.9 us
    reduce_scatter x1, waiting for transfers between devices, per_device(): lax.psum_scatter(partial_sum.astype(jnp.bfloat16), 'tensor', scatter_dime...  20.7 us
    dot_general x4, matrix products, add_product(): jnp.dot(activations, piece.reshape(piece.shape[0], -1), preferred_element...  20.2 us
  transfers between devices with their start and end apart: 8, of which 7 were waited for; matrix products, arithmetic and copies ran while one was open for 3% of the time, Pallas kernels for 0%

commit v1 on v0

--- a/solution.py
+++ b/solution.py
@@ -11,6 +11,16 @@
 ADAPTER_RANK = 16
 CONV = 4
 BLOCK = 128
+
+
+def ring_gather(x, axis, dim):
+    ways, here, step = (lax.axis_size(axis), lax.axis_index(axis), x.shape[dim])
+    dims = [n * ways if d == dim else n for d, n in enumerate(x.shape)]
+    full = lax.dynamic_update_slice_in_dim(jnp.zeros(dims, x.dtype), x, here * step, axis=dim)
+    for far in range(1, ways):
+        x = lax.ppermute(x, axis, [(d, (d + 1) % ways) for d in range(ways)])
+        full = lax.dynamic_update_slice_in_dim(full, x, (here - far) % ways * step, axis=dim)
+    return full
 
 
 def passed_along(array, axis, by):
@@ -106,7 +116,7 @@
 
     pieces = (
         lax.all_gather(gate_scanned_weight, "seq", axis=0, tiled=True),
-        lax.all_gather(mine_io, "seq", axis=0, tiled=True),
+        ring_gather(mine_io, "seq", 0),
         lax.all_gather(time_step_weight, "seq", axis=0, tiled=True),
         lax.all_gather(adapter_down_maps, "seq", axis=0, tiled=True),
     )

time: 962 us -> 931 us (0.968)
  waiting for transfers between devices: 799 us -> 670 us
  blocking collectives: 34.9 us -> 96.1 us
  starting transfers between devices: 3 us -> 24.6 us
  local copies, waits for them, and re-layouts: 52.5 us -> 67.2 us
    all_gather x1, waiting for transfers between devices: 557 us -> 438 us  [per_device(): lax.all_gather(gate_scanned_weight, 'seq', axis=0, tiled=True)]
    ppermute x0 -> x3, waiting for transfers between devices: none -> 84.8 us  [ring_gather(): x = lax.ppermute(x, axis, [(d, (d + 1) % ways) for d in range(ways)])]
    all_gather x1, blocking collectives: 17.2 us -> 76 us  [per_device(): lax.all_gather(time_step_weight, 'seq', axis=0, tiled=True)]
    all_gather x1 -> x0, waiting for transfers between devices: 56.1 us -> none  [per_device(): lax.all_gather(mine_io, 'seq', axis=0, tiled=True)]
    all_gather x1, waiting for transfers between devices: 40.3 us -> 0.02 us  [per_device(): lax.all_gather(adapter_down_maps, 'seq', axis=0, tiled=True)]
    ppermute x0 -> x3, starting transfers between devices: none -> 14.2 us  [ring_gather(): x = lax.ppermute(x, axis, [(d, (d + 1) % ways) for d in range(ways)])]
    dynamic_update_slice x0 -> x4, local copies, waits for them, and re-layouts: none -> 10.9 us  [the longest x3 7.55 us: ring_gather(): lax.dynamic_update_slice_in_dim(full, x, (here - far) % ways * step, axis...]
    unnamed x71 -> x69, local copies, waits for them, and re-layouts: 37 us -> 39.3 us
  transfers between devices with their start and end apart: 8 -> 10, of which waited for: 7 -> 8; matrix products, arithmetic and copies ran while one was open for 3% -> 5% of each run, Pallas kernels for 0% -> 0%
where the time goes in v1:
time: 931 us; the launch traced here: 930 us
  waiting for transfers between devices  670 us (72%)
  blocking collectives  96.1 us (10%)
  local copies, waits for them, and re-layouts  67.2 us (7%)
  matrix products  34.4 us (4%)
  starting transfers between devices  24.6 us (3%)
  other arithmetic  22.8 us (2%)
  between operations  15 us (2%)
    all_gather x1, waiting for transfers between devices, per_device(): lax.all_gather(gate_scanned_weight, 'seq', axis=0, tiled=True)  438 us
    ppermute x3, waiting for transfers between devices, ring_gather(): x = lax.ppermute(x, axis, [(d, (d + 1) % ways) for d in range(ways)])  84.8 us
    all_gather x1, waiting for transfers between devices, per_device(): gathered = lax.all_gather(gated, 'seq', axis=0, tiled=True)  82.3 us
    all_gather x1, blocking collectives, per_device(): lax.all_gather(time_step_weight, 'seq', axis=0, tiled=True)  76 us
    unnamed x69, local copies, waits for them, and re-layouts  39.3 us
    all_gather x1, waiting for transfers between devices, entering_2(): lax.all_gather(a.astype(kind), axis)  28.6 us
    reduce_scatter x1, waiting for transfers between devices, per_device(): lax.psum_scatter(partial_sum.astype(jnp.bfloat16), 'tensor', scatter_dime...  20.7 us
    dot_general x4, matrix products, add_product(): jnp.dot(activations, piece.reshape(piece.shape[0], -1), preferred_element...  19.6 us
  transfers between devices with their start and end apart: 10, of which 8 were waited for; matrix products, arithmetic and copies ran while one was open for 5% of the time, Pallas kernels for 0%

profile of v1, /device:TPU:0, one launch (start us, length us, event | category | flops | bytes accessed | tf_op | source)
XLA Modules:
  0.0 930.4 jit_solution(3200092755047495365)
XLA Ops:
  7.2 0.7 all-gather.8.cloned.1.call-update
  8.0 0.7 all-gather.6.cloned.1.call-update
  8.7 4.6 broadcast_in_dim.28
  13.3 3.3 constant_dynamic-update-slice_fusion.3
  16.7 3.0 collective-permute-start.1
  19.7 0.7 fusion.31
  21.0 0.6 copy.80
  21.6 0.6 copy.79
  22.8 0.7 constant_dynamic-slice_fusion.5
  23.6 42.6 %collective-permute-done.1 = bf16[1024,2,256]{2,1,0:T(2,128)(2,1)} collective-permute-done((bf16[1024,2,256]{2,1,0:T(2,128)(2,1)S(1)}, bf16[1024,2,256]{2,1,0:T(2,128)(2,1)}, u32[]{:S(2)}, u32[]{:S(2)}) %collective-permute-start.1) | collective-permute-done | bytes 1048608 | tf_op jit(solution)/shard_map/ppermute | solution.py:21
  66.3 11.2 %collective-permute-start.2 = (bf16[1024,2,256]{2,1,0:T(2,128)(2,1)}, bf16[1024,2,256]{2,1,0:T(2,128)(2,1)}, u32[]{:S(2)}, u32[]{:S(2)}) collective-permute-start(bf16[1024,2,256]{2,1,0:T(2,128)(2,1)} %collective-permute-done.1), channel_id=1, source_target_pairs={{0,4},{4,8},{8,12},{12,0},{1,5},{5,9},{9,13},{13,1},{2,6},{6,10},{... | collective-permute-start | bytes 3145736 | tf_op jit(solution)/shard_map/ppermute | solution.py:21
  77.4 76.0 %all_gather.22 = bf16[4096,32]{0,1:T(8,128)(2,1)S(1)} all-gather(bf16[1024,32]{0,1:T(8,128)(2,1)S(1)} %copy-done.13), channel_id=1, replica_groups=mesh['groups'=2,'seq'=4,'tensor'=4] {'seq'}, dimensions={0}, use_global_device_ids=true | all-gather | bytes 327680 | tf_op jit(solution)/shard_map/all_gather | solution.py:120
  153.4 0.7 convolution_add_fusion.2
  154.5 0.6 copy-done.10
  155.5 0.7 fusion.41
  156.1 0.7 copy.65
  157.2 3.9 copy.76
  161.6 0.6 slice_bitcast_fusion.3
  162.2 0.6 fusion.42
  162.8 2.9 constant_dynamic-update-slice_fusion.2
  165.7 2.9 constant_dynamic-update-slice_fusion.1
  168.7 42.2 %collective-permute-done.3 = bf16[1024,2,256]{2,1,0:T(2,128)(2,1)S(1)} collective-permute-done((bf16[1024,2,256]{2,1,0:T(2,128)(2,1)}, bf16[1024,2,256]{2,1,0:T(2,128)(2,1)S(1)}, u32[]{:S(2)}, u32[]{:S(2)}) %collective-permute-start.3) | collective-permute-done | bytes 1048608 | tf_op jit(solution)/shard_map/ppermute | solution.py:21
  210.9 1.7 constant_dynamic-update-slice_fusion
  212.6 2.9 copy.78
  215.5 1.3 fusion.16
  216.9 7.0 collective-permute-start.4
  223.9 2.3 fusion.17
  226.3 2.8 collective-permute-done.4
  229.3 1.5 multiply_convert_fusion.4
  230.8 0.7 fusion.40
  231.7 438.2 %all-gather.6.cloned.1.call-done = bf16[4096,2,2048]{2,1,0:T(2,128)(2,1)} async-done(((bf16[1024,2,2048]{2,1,0:T(2,128)(2,1)}), bf16[4096,2,2048]{2,1,0:T(2,128)(2,1)}) %all-gather.6.cloned.1.call-update) | async-done | bytes 33554448 | tf_op jit(solution)/shard_map/all_gather | solution.py:118
  669.9 23.2 %copy.75 = bf16[512,8,2,2048]{3,1,2,0:T(8,128)(2,1)} copy(bf16[512,8,2,2048]{3,2,1,0:T(2,128)(2,1)} %bitcast.126) | data formatting | bytes 67108864
  693.1 15.2 %fusion.43 = f32[256,4096]{1,0:T(8,128)S(1)} fusion(bf16[256,4096]{1,0:T(8,128)(2,1)S(1)} %copy-done, bf16[4096,4096]{1,0:T(8,128)(2,1)} %bitcast.127), kind=kOutput, calls=%fused_computation.110 | convolution fusion | flops 8589934592 | bytes 39845888 | tf_op jit(solution)/shard_map/dot_general | solution.py:113
  708.3 2.1 fusion.2
  710.4 3.3 copy.71
  713.9 3.2 collective-permute-start
  717.2 11.3 %collective-permute-done = bf16[3,2048]{0,1:T(8,128)(2,1)S(1)} collective-permute-done((bf16[3,2048]{0,1:T(8,128)(2,1)S(1)}, bf16[3,2048]{0,1:T(8,128)(2,1)S(1)}, u32[]{:S(2)}, u32[]{:S(2)}) %collective-permute-start) | collective-permute-done | bytes 12320 | tf_op jit(solution)/shard_map/ppermute | solution.py:29
  728.6 0.7 maximum_convert_fusion
  729.3 3.2 multiply_convert_fusion.2
  733.3 1.1 multiply_convert_fusion.1
  734.9 0.7 fusion.21
  735.6 1.6 add_convert_fusion
  737.4 0.8 copy.61
  738.2 13.2 %all-gather = bf16[4,1,32]{2,1,0:T(2,128)(2,1)S(1)} all-gather(bf16[1,1,32]{2,1,0:T(2,128)(2,1)S(1)} %fusion.35), channel_id=1, replica_groups=mesh['groups'=2,'seq'=4,'tensor'=4] {'seq'}, dimensions={0}, use_global_device_ids=true | all-gather | bytes 320 | tf_op jit(solution)/shard_map/all_gather | solution.py:35
  751.5 0.7 copy.63
  752.2 0.7 pad_exponential_fusion
  752.9 1.0 copy.73
  754.6 2.8 multiply_convert_fusion
  757.5 28.6 %all-gather.10.cloned.1.call-done = bf16[4,32,64,128]{3,2,1,0:T(8,128)(2,1)} async-done(((bf16[1,32,64,128]{3,2,1,0:T(8,128)(2,1)}), bf16[4,32,64,128]{3,2,1,0:T(8,128)(2,1)}) %all-gather.10.cloned.1.call-update) | async-done | bytes 2097168 | tf_op jit(solution)/shard_map/all_gather | solution.py:35
  786.3 1.2 copy-done.8
  787.5 2.9 fusion.19
  790.8 0.7 copy-done.7
  791.6 4.2 fusion.11
  795.8 1.5 fusion.10
  797.3 1.7 copy.69
  799.0 1.7 fusion.15
  800.8 82.3 %all-gather.12.cloned.1.call-done = bf16[1024,2048]{0,1:T(8,128)(2,1)} async-done(((bf16[256,2048]{0,1:T(8,128)(2,1)}), bf16[1024,2048]{0,1:T(8,128)(2,1)}) %all-gather.12.cloned.1.call-update) | async-done | bytes 4194320 | tf_op jit(solution)/shard_map/all_gather | solution.py:203
  883.1 3.0 fusion.1
  886.6 5.8 convolution_convert_fusion
  892.4 0.6 copy-done.27
  893.0 0.6 dynamic-slice
  894.3 6.8 all-reduce.2
  901.2 20.7 %reduce-scatter.2.cloned.1.call-done = bf16[256,1024]{1,0:T(8,128)(2,1)} async-done(((bf16[1024,1024]{1,0:T(8,128)(2,1)}), bf16[256,1024]{1,0:T(8,128)(2,1)}) %reduce-scatter.2.cloned.1.call-update) | async-done | bytes 524304 | tf_op jit(solution)/shard_map/reduce_scatter | solution.py:208
  921.9 2.0 multiply_convert_fusion.3
  (98 shorter events, 7.2 us)
Async XLA Ops:
  7.2 146.3 %copy-start = (bf16[256,4096]{1,0:T(8,128)(2,1)S(1)}, bf16[256,4096]{1,0:T(8,128)(2,1)}, u32[]{:S(2)}) copy-start(bf16[256,4096]{1,0:T(8,128)(2,1)} %param.19) | copy-start | bytes 6291460
  7.2 216.8 %all-gather.8.cloned.1.call-start = ((), (), s32[]{:S(2)}) async-start(), calls=%async_computation.2 | async-start | bytes 2621440 | tf_op jit(solution)/shard_map/all_gather | solution.py:121
  7.9 662.0 %all-gather.6.cloned.1.call-start = ((), (), s32[]{:S(2)}) async-start(), calls=%async_computation.1 | async-start | bytes 41943040 | tf_op jit(solution)/shard_map/all_gather | solution.py:118
  8.7 777.4 %all-gather.10.cloned.1.call-start = ((), (), s32[]{:S(2)}) async-start(), calls=%async_computation.3 | async-start | bytes 2621440 | tf_op jit(solution)/shard_map/all_gather | solution.py:35
  13.3 6.4 copy-start.26
  13.3 64.1 %copy-start.13 = (bf16[1024,32]{0,1:T(8,128)(2,1)S(1)}, bf16[1024,32]{0,1:T(8,128)(2,1)}, u32[]{:S(2)}) copy-start(bf16[1024,32]{0,1:T(8,128)(2,1)} %param.23) | copy-start | bytes 196612
  13.3 140.1 %copy-start.22 = (f32[32]{0:T(128)S(1)}, f32[32]{0:T(128)}, u32[]{:S(2)}) copy-start(f32[32]{0:T(128)} %param.30) | copy-start | bytes 388
  16.7 137.5 %copy-start.24 = (f32[16,32]{1,0:T(8,128)S(1)}, f32[16,32]{1,0:T(8,128)}, u32[]{:S(2)}) copy-start(f32[16,32]{1,0:T(8,128)} %param.31) | copy-start | bytes 6148
  16.7 137.5 %copy-start.25 = (s32[256]{0:T(256)S(1)}, s32[256]{0:T(256)}, u32[]{:S(2)}) copy-start(s32[256]{0:T(256)} %param.20) | copy-start | bytes 3076
  16.7 49.6 %collective-permute-start.1 = (bf16[1024,2,256]{2,1,0:T(2,128)(2,1)S(1)}, bf16[1024,2,256]{2,1,0:T(2,128)(2,1)}, u32[]{:S(2)}, u32[]{:S(2)}) collective-permute-start(bf16[1024,2,256]{2,1,0:T(2,128)(2,1)S(1)} %get-tuple-element.55), channel_id=1, source_target_pairs={{0,4},{4,8},{8,12},{12,0},{1,5},{5,9},{9,13},{13,1},{2,6},{6,10},{... | collective-permute-start | bytes 3145736 | tf_op jit(solution)/shard_map/ppermute | solution.py:21
  23.6 133.2 %copy-start.17 = (bf16[3,2048]{1,0:T(4,128)(2,1)S(1)}, bf16[3,2048]{1,0:T(4,128)(2,1)}, u32[]{:S(2)}) copy-start(bf16[3,2048]{1,0:T(4,128)(2,1)} %param.28) | copy-start | bytes 36868
  66.3 94.8 %collective-permute-start.2 = (bf16[1024,2,256]{2,1,0:T(2,128)(2,1)}, bf16[1024,2,256]{2,1,0:T(2,128)(2,1)}, u32[]{:S(2)}, u32[]{:S(2)}) collective-permute-start(bf16[1024,2,256]{2,1,0:T(2,128)(2,1)} %collective-permute-done.1), channel_id=1, source_target_pairs={{0,4},{4,8},{8,12},{12,0},{1,5},{5,9},{9,13},{13,1},{2,6},{6,10},{... | collective-permute-start | bytes 3145736 | tf_op jit(solution)/shard_map/ppermute | solution.py:21
  154.5 0.6 copy-start.10
  157.1 5.0 copy-start.16
  161.0 49.9 %collective-permute-start.3 = (bf16[1024,2,256]{2,1,0:T(2,128)(2,1)}, bf16[1024,2,256]{2,1,0:T(2,128)(2,1)S(1)}, u32[]{:S(2)}, u32[]{:S(2)}) collective-permute-start(bf16[1024,2,256]{2,1,0:T(2,128)(2,1)} %collective-permute-done.2), channel_id=1, source_target_pairs={{0,4},{4,8},{8,12},{12,0},{1,5},{5,9},{9,13},{13,1},{2,6},{6,10},{... | collective-permute-start | bytes 3145736 | tf_op jit(solution)/shard_map/ppermute | solution.py:21
  216.9 12.2 %collective-permute-start.4 = (bf16[3,512]{0,1:T(8,128)(2,1)S(1)}, bf16[3,512]{0,1:T(8,128)(2,1)S(1)}, u32[]{:S(2)}, u32[]{:S(2)}) collective-permute-start(bf16[3,512]{0,1:T(8,128)(2,1)S(1)} %slice.130), channel_id=1, source_target_pairs={{0,4},{4,8},{8,12},{1,5},{5,9},{9,13},{2,6},{6,10},{10,14},{3,7},{... | collective-permute-start | bytes 9224 | tf_op jit(solution)/shard_map/ppermute | solution.py:29
  693.1 15.2 %copy-start.6 = (bf16[32,8,2,2048]{3,1,2,0:T(8,128)(2,1)S(1)}, bf16[32,8,2,2048]{3,1,2,0:T(8,128)(2,1)}, u32[]{:S(2)}) copy-start(bf16[32,8,2,2048]{3,1,2,0:T(8,128)(2,1)} %copy.76) | copy-start | bytes 6291460
  713.7 14.9 %copy-start.3 = (bf16[256,4096]{0,1:T(8,128)(2,1)}, bf16[256,4096]{0,1:T(8,128)(2,1)S(1)}, u32[]{:S(2)}) copy-start(bf16[256,4096]{0,1:T(8,128)(2,1)S(1)} %copy.71) | copy-start | bytes 6291460
  713.9 14.6 %collective-permute-start = (bf16[3,2048]{0,1:T(8,128)(2,1)S(1)}, bf16[3,2048]{0,1:T(8,128)(2,1)S(1)}, u32[]{:S(2)}, u32[]{:S(2)}) collective-permute-start(bf16[3,2048]{0,1:T(8,128)(2,1)S(1)} %slice_bitcast_fusion.2), channel_id=1, source_target_pairs={{0,4},{4,8},{8,12},{1,5},{5,9},{9,13},{2,6},{6,10},{10,14},{3,7},{... | collective-permute-start | bytes 36872 | tf_op jit(solution)/shard_map/ppermute | solution.py:29
  728.6 0.7 copy-start.14
  728.6 0.7 copy-start.15
  732.5 0.8 copy-start.11
  734.8 0.7 copy-start.19
  734.8 0.7 copy-start.20
  735.5 1.9 copy-start.2
  735.6 15.9 %copy-start.9 = (f32[2,128,32]{2,1,0:T(8,128)S(1)}, f32[2,128,32]{2,1,0:T(8,128)}, u32[]{:S(2)}) copy-start(f32[2,128,32]{2,1,0:T(8,128)} %get-tuple-element.62) | copy-start | bytes 98308
  737.4 145.7 %all-gather.12.cloned.1.call-start = ((), (), s32[]{:S(2)}) async-start(), calls=%async_computation.4 | async-start | bytes 5242880 | tf_op jit(solution)/shard_map/all_gather | solution.py:203
  786.2 1.2 copy-start.8
  786.2 1.2 copy-start.21
  790.3 1.2 copy-start.7
  791.6 4.2 copy-start.5
  791.6 4.2 copy-start.12
  797.3 1.7 copy-start.4
  799.0 84.1 %copy-start.18 = (f32[2048]{0:T(1024)S(1)}, f32[2048]{0:T(1024)}, u32[]{:S(2)}) copy-start(f32[2048]{0:T(1024)} %param.34) | copy-start | bytes 24580
  800.7 121.2 %reduce-scatter.2.cloned.1.call-start = ((), (), s32[]{:S(2)}) async-start(), calls=%async_computation.5 | async-start | bytes 2621440 | tf_op jit(solution)/shard_map/reduce_scatter | solution.py:208
  883.1 3.4 copy-start.23
  886.6 37.3 %copy-start.1 = (bf16[256,4096]{1,0:T(8,128)(2,1)S(1)}, bf16[256,4096]{1,0:T(8,128)(2,1)}, u32[]{:S(2)}) copy-start(bf16[256,4096]{1,0:T(8,128)(2,1)} %param.19) | copy-start | bytes 6291460
  892.4 0.7 copy-start.27
Sparse Core Ops, SparseCore 0:
  9.6 69.5 all-gather.7
  80.7 589.1 all-gather.5
  737.4 48.6 all-gather.9
  800.8 82.2 all-gather.11
  892.5 29.3 reduce-scatter.1
